TPU v7x, 32 devices: a whole 2x2x4 slice. The times are simulated.
32 devices in a mesh: parts: 2 (over x), chan: 4 (over y, core), tmpl: 4 (over z).
Axes of the slice: x: 2, y: 2, z: 4, core: 2. Of those that a mesh axis runs over, the one named last changes fastest.
Arguments:
- raw_traces: float32 [4096, 2816], P(('chan', 'tmpl'), 'parts'), parts along dimension 1, may hold values from -50 to 50
- filter_taps: float32 [129], replicated, may hold values from -0.5 to 0.5
- templates: bfloat16 [32, 200, 4096], P('tmpl', None, 'chan'), may hold values from -6 to 6
- offsets: int32 [32], P('tmpl'), may hold values from 0 to 56
- channel_mask: int32 [32, 4096], P('tmpl'), may hold values from 0 to 1, as said below
Outputs:
- detection: float32 [32, 2048], P('tmpl', ('parts', 'chan')), parts along dimension 1
There are 2 independent parts, one for each index of `parts`. A program takes and returns all parts, laid end to end along the dimension named above; an argument that names none is the same for every part. Nothing has to cross between parts.
Inputs may be any that keep to these rules, and one draw needn't show every extreme that they name: `channel_mask`: each template uses one contiguous run of 4 or more blocks of 128 channels, starting and ending at multiples of 128; some template uses all channels.
All inputs are finite; a program needn't handle non-finite values.
Results may differ from a plain program's by a relative error of at most 0.004.
Values may be sent and summed in bfloat16 or wider, within the bound.
A program may use at most 128 MiB of HBM per device.

v0:
```python
import functools

import jax
import jax.numpy as jnp
from jax import lax
from jax.experimental import pallas as pl
from jax.experimental.pallas import tpu as pltpu
from jax.sharding import PartitionSpec as P

SPAN = 256
BLK = 256
LANE = 128
MESH = pl.DeviceIdType.MESH
PIECES = 1


def left(x, count):
    size = x.shape[-1]
    count = count % size
    return x if count == 0 else pltpu.roll(x, size - count, x.ndim - 1)


def kernel(
    ntm, nch, lend, raw_hbm, taps_hbm, tmpl_hbm, mask_hbm, offs_hbm, out_ref,
    taps_ref, offs_ref, raw, tap_row, tmpl, mask, skewed, shaped, rall, prod, qacc, units, num_out, en_out,
    num_in, en_in, guest, gacc, gsum, load_sem, raw_sem, recv_sem, right_sem, left_sem,
    unit_right, unit_left, unit_recv, num_send, num_recv, en_send, en_recv, guest_sem, gsum_sem,
):
    z = lax.axis_index("tmpl")
    c = lax.axis_index("chan")
    rows = raw.shape[0]
    group, tlen, local = tmpl.shape
    nblk = rall.shape[0]
    total = nblk * BLK
    unit = min(LANE, rows)
    nun = rows // unit

    def load_raw(n, first):
        at = pl.ds(0, BLK + LANE) if first else pl.ds(pl.multiple_of(n * BLK + LANE, LANE), BLK)
        return pltpu.make_async_copy(raw_hbm.at[:, at], raw.at[:, at], raw_sem.at[n])

    load_taps = pltpu.make_async_copy(taps_hbm, taps_ref, load_sem.at[2])
    load_taps.start()
    for n in range(nblk):
        load_raw(n, n == 0).start()
    loads = [
        pltpu.make_async_copy(tmpl_hbm, tmpl, load_sem.at[0]),
        pltpu.make_async_copy(
            mask_hbm.at[:, pl.ds(pl.multiple_of(c * local, LANE), local)], mask, load_sem.at[1]
        ),
        pltpu.make_async_copy(offs_hbm, offs_ref, load_sem.at[3]),
    ]
    for item in loads:
        item.start()

    barrier = pltpu.get_barrier_semaphore()
    @pl.when(z < ntm - 1)
    def _():
        pl.semaphore_signal(
            barrier, inc=1, device_id={"tmpl": lax.rem(z + 1, ntm)}, device_id_type=MESH
        )

    @pl.when(z > 0)
    def _():
        pl.semaphore_signal(
            barrier, inc=1, device_id={"tmpl": lax.rem(z - 1 + ntm, ntm)}, device_id_type=MESH
        )

    for d in range(1, nch):
        pl.semaphore_signal(
            barrier, inc=1, device_id={"chan": lax.rem(c + d, nch)}, device_id_type=MESH
        )

    tap_row[...] = jnp.zeros_like(tap_row)
    load_taps.wait()
    tap_row[:, : taps_ref.shape[1]] = taps_ref[...]
    band = pltpu.roll(
        jnp.broadcast_to(tap_row[...], (LANE, 2 * LANE)), 0, 1, stride=1, stride_axis=0
    )
    band_hi = band.astype(jnp.bfloat16)
    band_lo = (band - band_hi.astype(jnp.float32)).astype(jnp.bfloat16)
    qacc[...] = jnp.zeros_like(qacc)
    is_end = (z == 0) | (z == ntm - 1)
    is_helper = (z == 1) | (z == ntm - 2)
    inward = jnp.where(z == 0, 1, ntm - 2)
    outward = jnp.where(z == 1, 0, ntm - 1)
    if lend:
        @pl.when(is_end)
        def _():
            at = pl.ds(pl.multiple_of(inward * rows, rows), rows)
            for n in range(nblk):
                rall[n, at, :] = jnp.zeros((rows, BLK), jnp.bfloat16)

    load_raw(0, True).wait()

    def chunk(src, n):
        return rall.at[n, pl.ds(pl.multiple_of(src * rows, rows), rows), :]

    def hop(src, n, h, sems, step):
        height = rows // PIECES
        at = pl.ds(pl.multiple_of(src * rows + h * height, height), height)
        return pltpu.make_async_remote_copy(
            src_ref=rall.at[n, at, :],
            dst_ref=rall.at[n, at, :],
            send_sem=sems.at[src, n * PIECES + h],
            recv_sem=recv_sem.at[src, n * PIECES + h],
            device_id={"tmpl": lax.rem(z + step + ntm, ntm)},
            device_id_type=MESH,
        )

    def contract(a, b):
        return lax.dot_general(
            a, b, (((1,), (1,)), ((), ())), preferred_element_type=jnp.float32
        )

    def fir(n, carry):
        x = raw[:, pl.ds(pl.multiple_of(n * BLK, BLK), BLK + LANE)]
        hi = x.astype(jnp.bfloat16)
        lo = (x - hi.astype(jnp.float32)).astype(jnp.bfloat16)
        for half in range(BLK // LANE):
            a = hi[:, half * LANE : half * LANE + 2 * LANE]
            b = lo[:, half * LANE : half * LANE + 2 * LANE]
            y = contract(a, band_hi) + (contract(b, band_hi) + contract(a, band_lo))
            y = y.astype(jnp.bfloat16)
            rall[
                n, pl.ds(pl.multiple_of(z * rows, rows), rows), half * LANE : half * LANE + LANE
            ] = y
            y = y.astype(jnp.float32)
            y = y * y
            at = pl.ds(pl.multiple_of(n * BLK + half * LANE, LANE), LANE)
            for u in range(nun):
                units[z, u : u + 1, at] = jnp.sum(
                    y[u * unit : (u + 1) * unit], axis=0, keepdims=True
                )

        return carry

    def send_own(n, carry):
        @pl.when(z < ntm - 1 - lend)
        def _():
            for h in range(PIECES):
                hop(z, n, h, right_sem, 1).start()

        @pl.when(z > lend)
        def _():
            for h in range(PIECES):
                hop(z, n, h, left_sem, -1).start()

        return carry

    def fir_next(n, carry):
        load_raw(n, False).wait()
        return fir(n, carry)

    def unit_hop(src, sems, step):
        return pltpu.make_async_remote_copy(
            src_ref=units.at[src],
            dst_ref=units.at[src],
            send_sem=sems.at[src],
            recv_sem=unit_recv.at[src],
            device_id={"tmpl": lax.rem(z + step + ntm, ntm)},
            device_id_type=MESH,
        )

    fir(0, 0)
    pl.semaphore_wait(
        barrier, jnp.where(z < ntm - 1, 1, 0) + jnp.where(z > 0, 1, 0) + (nch - 1)
    )
    send_own(0, 0)
    lax.fori_loop(1, nblk, fir_next, 0)

    @pl.when(z < ntm - 1)
    def _():
        unit_hop(z, unit_right, 1).start()

    @pl.when(z > 0)
    def _():
        unit_hop(z, unit_left, -1).start()

    lax.fori_loop(1, nblk, send_own, 0)

    for item in loads:
        item.wait()

    def shape_cols(i, carry):
        cols = pl.ds(pl.multiple_of(i * LANE, LANE), LANE)
        flags = mask[:, cols].astype(jnp.float32)
        for k in range(group):
            v = tmpl[k, :, cols].astype(jnp.float32)
            power = jnp.mean(v * v, axis=0, keepdims=True)
            scale = flags[k : k + 1, :] / jnp.sqrt(power + 1e-06)
            skewed[pl.ds(k, tlen, stride=group), :] = v * scale
        shaped[:, cols] = skewed[...].astype(jnp.bfloat16)
        return carry

    lax.fori_loop(0, local // LANE, shape_cols, 0)

    cut = min(LANE, tlen) * group
    parts = [(0, cut), (cut, tlen * group - cut)]

    def lend_copy(p, peer):
        cols = pl.ds(pl.multiple_of(inward * rows, rows), rows)
        lines = pl.ds(*parts[p])
        return pltpu.make_async_remote_copy(
            src_ref=shaped.at[lines, cols],
            dst_ref=guest.at[lines, :],
            send_sem=guest_sem.at[0, p],
            recv_sem=guest_sem.at[1, p],
            device_id={"tmpl": peer},
            device_id_type=MESH,
        )

    def gsum_copy(peer):
        return pltpu.make_async_remote_copy(
            src_ref=gacc.at[:, pl.ds(BLK, total)],
            dst_ref=gsum,
            send_sem=gsum_sem.at[0],
            recv_sem=gsum_sem.at[1],
            device_id={"tmpl": peer},
            device_id_type=MESH,
        )

    if lend:
        @pl.when(is_end)
        def _():
            lend_copy(0, inward).start()
            lend_copy(1, inward).start()

    offs = jnp.zeros((group, 1), jnp.int32)
    index = lax.broadcasted_iota(jnp.int32, (group, 1), 0)
    for k in range(group):
        offs = jnp.where(index == k, offs_ref[k], offs)

    def shift_rows(x):
        amount = jnp.broadcast_to(offs, x.shape)
        bit = 1
        while bit < SPAN - tlen + 1:
            x = jnp.where((amount & bit) != 0, left(x, bit), x)
            bit *= 2
        return x

    def spread(x, own_ref, in_ref, send, recv):
        lag = own_ref.shape[2]
        for j in range(nch):
            own_ref[j] = x[:, j * lag : (j + 1) * lag]
        for d in range(1, nch):
            other = lax.rem(c + d, nch)
            pltpu.make_async_remote_copy(
                src_ref=own_ref.at[other],
                dst_ref=in_ref.at[d],
                send_sem=send.at[d],
                recv_sem=recv.at[d],
                device_id={"chan": other},
                device_id_type=MESH,
            ).start()

    def collect(own_ref, in_ref, send, recv):
        value = own_ref[c]
        for d in range(1, nch):
            pltpu.make_async_remote_copy(
                src_ref=own_ref.at[lax.rem(c + d, nch)],
                dst_ref=in_ref.at[d],
                send_sem=send.at[d],
                recv_sem=recv.at[d],
                device_id={"chan": lax.rem(c + d, nch)},
                device_id_type=MESH,
            ).wait()
            value = value + in_ref[d]
        return value

    def unit_arrive(d):
        @pl.when(z - d >= 0)
        def _():
            src = lax.rem(z - d + ntm, ntm)
            unit_hop(src, unit_right, 1).wait_recv()

            @pl.when(z < ntm - 1)
            def _():
                unit_hop(src, unit_right, 1).start()

        @pl.when(z + d < ntm)
        def _():
            src = lax.rem(z + d, ntm)
            unit_hop(src, unit_left, -1).wait_recv()

            @pl.when(z > 0)
            def _():
                unit_hop(src, unit_left, -1).start()

    def send_energy():
        masses = jnp.zeros((group, total), jnp.float32)
        for s in range(ntm):
            for u in range(nun):
                at = s * rows + u * unit
                flag = mask[:, at : at + 1].astype(jnp.float32)
                masses = masses + flag * units[s, u : u + 1, :]
        window, width, place, energy = masses, 1, 0, None
        while width <= tlen:
            if tlen & width:
                piece = left(window, place)
                energy = piece if energy is None else energy + piece
                place += width
            window = window + left(window, width)
            width *= 2
        spread(shift_rows(energy), en_out, en_in, en_send, en_recv)

    def arrive(d, n):
        near = lend if d == 1 else 0

        @pl.when((z - d >= 0) & (z < ntm - near))
        def _():
            src = lax.rem(z - d + ntm, ntm)
            for h in range(PIECES):
                hop(src, n, h, right_sem, 1).wait_recv()

                @pl.when(z < ntm - 1)
                def _():
                    hop(src, n, h, right_sem, 1).start()

        @pl.when((z + d < ntm) & (z >= near))
        def _():
            src = lax.rem(z + d, ntm)
            for h in range(PIECES):
                hop(src, n, h, left_sem, -1).wait_recv()

                @pl.when(z > 0)
                def _():
                    hop(src, n, h, left_sem, -1).start()

    def skew(n, weights, samples, acc, begin, end):
        prod[: weights.shape[0], :] = jnp.dot(
            weights, samples, preferred_element_type=jnp.float32
        )
        blank = jnp.zeros((group, LANE), jnp.float32)
        total_acc = jnp.zeros((group, 2 * BLK), jnp.float32)

        def row(tap):
            if tap < begin or tap >= end:
                return None
            line = (tap - begin) * group
            return prod[line : line + group, :]

        for g in range(min(LANE, tlen)):
            low, high = row(g), row(g + LANE)
            if low is None and high is None:
                continue
            carry_in, first, second = blank, blank, blank
            if low is not None:
                first, second = low[:, :LANE], low[:, LANE:]
            if high is not None:
                carry_in = high[:, :LANE]
                first = high[:, LANE:] if low is None else first + high[:, LANE:]
            wide = jnp.concatenate([blank, carry_in, first, second], axis=1)
            total_acc = total_acc + left(wide, g)
        at = pl.ds(pl.multiple_of(n * BLK, BLK), 2 * BLK)
        acc[:, at] = acc[:, at] + total_acc

    def guest_block(p, n, carry):
        line, count = parts[p]
        weights = guest[line : line + count, :]
        skew(n, weights, chunk(z, n)[...], gacc, line // group, (line + count) // group)
        return carry

    def block(n, carry):
        for d in range(max(1, ntm // 2), ntm):
            arrive(d, n)

        @pl.when(n == min(1, nblk - 1))
        def _():
            for d in range(max(1, ntm // 2), ntm):
                unit_arrive(d)
            send_energy()

        if lend:
            @pl.when((n == nblk - 1) & is_helper)
            def _():
                gacc[...] = jnp.zeros_like(gacc)
                lend_copy(0, outward).wait_recv()
                lax.fori_loop(0, nblk, functools.partial(guest_block, 0), 0)

        skew(n, shaped[...], rall[n], qacc, 0, tlen)
        return carry

    def step(d):
        def body(n, carry):
            arrive(d, n)

            @pl.when(n == 0)
            def _():
                unit_arrive(d)

            return carry

        lax.fori_loop(0, nblk, body, 0)

    for d in range(1, max(1, ntm // 2)):
        step(d)
    lax.fori_loop(0, nblk, block, 0)

    if lend:
        @pl.when(is_helper)
        def _():
            lend_copy(1, outward).wait_recv()
            lax.fori_loop(0, nblk, functools.partial(guest_block, 1), 0)
            gsum_copy(outward).start()

        @pl.when(is_end)
        def _():
            gsum_copy(inward).wait_recv()
            qacc[:, BLK:] = qacc[:, BLK:] + gsum[...]

    spread(shift_rows(qacc[:, BLK:]), num_out, num_in, num_send, num_recv)
    energy = collect(en_out, en_in, en_send, en_recv)
    numerator = collect(num_out, num_in, num_send, num_recv)
    out_ref[...] = numerator / jnp.sqrt(energy)

    def drain(n, carry):
        for s in range(ntm):
            @pl.when((s <= z) & (z < ntm - 1) & ((s != z) | (z < ntm - 1 - lend)))
            def _():
                for h in range(PIECES):
                    hop(s, n, h, right_sem, 1).wait_send()

            @pl.when((s >= z) & (z > 0) & ((s != z) | (z > lend)))
            def _():
                for h in range(PIECES):
                    hop(s, n, h, left_sem, -1).wait_send()

        return carry

    lax.fori_loop(0, nblk, drain, 0)
    for s in range(ntm):
        @pl.when((s <= z) & (z < ntm - 1))
        def _():
            unit_hop(s, unit_right, 1).wait_send()

        @pl.when((s >= z) & (z > 0))
        def _():
            unit_hop(s, unit_left, -1).wait_send()

    if lend:
        @pl.when(is_end)
        def _():
            lend_copy(0, inward).wait_send()
            lend_copy(1, inward).wait_send()

        @pl.when(is_helper)
        def _():
            gsum_copy(outward).wait_send()


def shards(raw_traces, filter_taps, templates, offsets, channel_mask):
    ntm = lax.axis_size("tmpl")
    nch = lax.axis_size("chan")
    rows, length = raw_traces.shape
    group, tlen, local = templates.shape
    nblk = (length - filter_taps.shape[0] + 1) // BLK
    total = nblk * BLK
    lag = (total - SPAN) // nch
    nun = rows // min(LANE, rows)
    lend = int(ntm >= 4 and rows % LANE == 0 and tlen > LANE)
    f32, bf16, dma = jnp.float32, jnp.bfloat16, pltpu.SemaphoreType.DMA
    any_spec = pl.BlockSpec(memory_space=pl.ANY)
    vmem_spec = pl.BlockSpec(memory_space=pltpu.VMEM)
    return pl.pallas_call(
        functools.partial(kernel, ntm, nch, lend),
        out_shape=jax.ShapeDtypeStruct((group, lag), f32),
        in_specs=[
            any_spec, any_spec, any_spec, any_spec, any_spec,
        ],
        out_specs=vmem_spec,
        scratch_shapes=[
            pltpu.VMEM((1, filter_taps.shape[0]), f32),
            pltpu.SMEM((group,), jnp.int32),
            pltpu.VMEM((rows, length), f32),
            pltpu.VMEM((1, 2 * LANE), f32),
            pltpu.VMEM((group, tlen, local), bf16),
            pltpu.VMEM((group, local), jnp.int32),
            pltpu.VMEM((group * tlen, LANE), f32),
            pltpu.VMEM((group * tlen, local), bf16),
            pltpu.VMEM((nblk, local, BLK), bf16),
            pltpu.VMEM((group * tlen, BLK), f32),
            pltpu.VMEM((group, BLK + total), f32),
            pltpu.VMEM((ntm, nun, total), f32),
            pltpu.VMEM((nch, group, lag), f32),
            pltpu.VMEM((nch, group, lag), f32),
            pltpu.VMEM((nch, group, lag), f32),
            pltpu.VMEM((nch, group, lag), f32),
            pltpu.VMEM((group * tlen, rows if lend else LANE), bf16),
            pltpu.VMEM((group, BLK + total), f32),
            pltpu.VMEM((group, total), f32),
            dma((4,)),
            dma((nblk,)),
            dma((ntm, nblk * PIECES)),
            dma((ntm, nblk * PIECES)),
            dma((ntm, nblk * PIECES)),
            dma((ntm,)),
            dma((ntm,)),
            dma((ntm,)),
            dma((nch,)),
            dma((nch,)),
            dma((nch,)),
            dma((nch,)),
            dma((2, 2)),
            dma((2,)),
        ],
        compiler_params=pltpu.CompilerParams(
            collective_id=0, has_side_effects=True, vmem_limit_bytes=60 * 1024 * 1024
        ),
    )(raw_traces, filter_taps.reshape(1, -1), templates, channel_mask, offsets)


def solution(mesh):
    placed = (
        P(("chan", "tmpl"), "parts"),
        P(),
        P("tmpl", None, "chan"),
        P("tmpl"),
        P("tmpl", None),
    )
    return jax.shard_map(
        shards, mesh=mesh, in_specs=placed, out_specs=P("tmpl", ("parts", "chan")), check_vma=False
    )
```

profile of v0, /device:TPU:0, one launch (start us, length us, event | category | flops | bytes accessed | tf_op | source)
XLA Modules:
  0.0 49.8 jit_solution(17558636247473901384)
XLA Ops:
  0.0 48.5 %shard_map.55 = f32[8,256]{1,0:T(8,128)} custom-call(f32[256,1408]{1,0:T(8,128)} %raw_hbm.1, f32[1,129]{1,0:T(1,128)} %bitcast.1, bf16[8,200,1024]{2,1,0:T(8,128)(2,1)} %tmpl_hbm.1, s32[8,4096]{1,0:T(8,128)} %mask_hbm.1, s32[8]{0:T(128)} %offs_hbm.1), custom_call_target="tpu_custom_call" | custom-call | tf_op jit(solution)/shard_map/pallas_call | solution.py:465
  48.5 1.3 %copy.7 = f32[8,256]{1,0:T(8,128)} copy(f32[8,256]{1,0:T(8,128)} %shard_map.55) | data formatting | bytes 16384
where the time goes:
time: 50 us; the launch traced here: 49.8 us
  Pallas kernels  48.5 us (97%)
  local copies, waits for them, and re-layouts  1.3 us (3%)
    pallas_call x1, Pallas kernels, shards(): pl.pallas_call(functools.partial(kernel, ntm, nch, lend), out_shape=jax.S...  48.5 us
    unnamed x1, local copies, waits for them, and re-layouts  1.3 us

commit v1 on v0

--- a/solution.py
+++ b/solution.py
@@ -12,6 +12,8 @@
 LANE = 128
 MESH = pl.DeviceIdType.MESH
 PIECES = 1
+LEAD = 3
+LOANS = 4
 
 
 def left(x, count):
@@ -21,19 +23,30 @@
 
 
 def kernel(
-    ntm, nch, lend, raw_hbm, taps_hbm, tmpl_hbm, mask_hbm, offs_hbm, out_ref,
+    ntm, nch, npt, lend, share, lead, raw_hbm, taps_hbm, tmpl_hbm, mask_hbm, offs_hbm, out_ref,
     taps_ref, offs_ref, raw, tap_row, tmpl, mask, skewed, shaped, rall, prod, qacc, units, num_out, en_out,
-    num_in, en_in, guest, gacc, gsum, load_sem, raw_sem, recv_sem, right_sem, left_sem,
-    unit_right, unit_left, unit_recv, num_send, num_recv, en_send, en_recv, guest_sem, gsum_sem,
+    num_in, en_in, guest, gacc, guest_out, guest_in, own_offs, guest_offs,
+    load_sem, raw_sem, recv_sem, right_sem, left_sem,
+    unit_right, unit_left, unit_recv, num_send, num_recv, en_send, en_recv,
+    loan_send, loan_recv, relay_send, relay_recv, offs_sem, guest_send, guest_recv,
 ):
     z = lax.axis_index("tmpl")
     c = lax.axis_index("chan")
+    p = lax.axis_index("parts")
     rows = raw.shape[0]
     group, tlen, local = tmpl.shape
     nblk = rall.shape[0]
     total = nblk * BLK
     unit = min(LANE, rows)
     nun = rows // unit
+    side = ntm // 2 if ntm % 2 == 0 and (ntm // 2 * rows) % LANE == 0 else ntm
+    width = side * rows
+    near = lax.div(z, side)
+    is_end = (z == 0) | (z == ntm - 1)
+    is_helper = (z == 1) | (z == ntm - 2)
+    inward = jnp.where(z == 0, 1, ntm - 2)
+    outward = jnp.where(z == 1, 0, ntm - 1)
+    lent = jnp.where(z < ntm - 2, 2, ntm - 3) if ntm != 4 else jnp.where(z < 2, 2, 1)
 
     def load_raw(n, first):
         at = pl.ds(0, BLK + LANE) if first else pl.ds(pl.multiple_of(n * BLK + LANE, LANE), BLK)
@@ -71,6 +84,20 @@
             barrier, inc=1, device_id={"chan": lax.rem(c + d, nch)}, device_id_type=MESH
         )
 
+    if lend:
+        @pl.when(is_end)
+        def _():
+            for d in range(1, nch):
+                pl.semaphore_signal(
+                    barrier, inc=1,
+                    device_id={"chan": lax.rem(c + d, nch), "tmpl": inward}, device_id_type=MESH,
+                )
+
+        for e in range(1, share):
+            pl.semaphore_signal(
+                barrier, inc=1, device_id={"parts": lax.rem(p + e, npt)}, device_id_type=MESH
+            )
+
     tap_row[...] = jnp.zeros_like(tap_row)
     load_taps.wait()
     tap_row[:, : taps_ref.shape[1]] = taps_ref[...]
@@ -80,16 +107,16 @@
     band_hi = band.astype(jnp.bfloat16)
     band_lo = (band - band_hi.astype(jnp.float32)).astype(jnp.bfloat16)
     qacc[...] = jnp.zeros_like(qacc)
-    is_end = (z == 0) | (z == ntm - 1)
-    is_helper = (z == 1) | (z == ntm - 2)
-    inward = jnp.where(z == 0, 1, ntm - 2)
-    outward = jnp.where(z == 1, 0, ntm - 1)
     if lend:
         @pl.when(is_end)
         def _():
-            at = pl.ds(pl.multiple_of(inward * rows, rows), rows)
+            at = pl.ds(pl.multiple_of(lent * rows, rows), rows)
             for n in range(nblk):
                 rall[n, at, :] = jnp.zeros((rows, BLK), jnp.bfloat16)
+
+        @pl.when(is_helper)
+        def _():
+            gacc[...] = jnp.zeros_like(gacc)
 
     load_raw(0, True).wait()
 
@@ -135,16 +162,38 @@
 
         return carry
 
+    def send_right(src, n):
+        for h in range(PIECES):
+            hop(src, n, h, right_sem, 1).start()
+
+    def send_left(src, n):
+        for h in range(PIECES):
+            hop(src, n, h, left_sem, -1).start()
+
+    goes_right = z < ntm - 1
+    goes_left = z > 0
+    held_right = (z == 1) & (lead < nblk)
+    held_left = (z == ntm - 2) & (lead < nblk)
+
     def send_own(n, carry):
-        @pl.when(z < ntm - 1 - lend)
-        def _():
-            for h in range(PIECES):
-                hop(z, n, h, right_sem, 1).start()
-
-        @pl.when(z > lend)
-        def _():
-            for h in range(PIECES):
-                hop(z, n, h, left_sem, -1).start()
+        @pl.when(goes_right & ((n < lead) | jnp.logical_not(held_right)))
+        def _():
+            send_right(z, n)
+
+        @pl.when(goes_left & ((n < lead) | jnp.logical_not(held_left)))
+        def _():
+            send_left(z, n)
+
+        return carry
+
+    def send_held(n, carry):
+        @pl.when(held_right)
+        def _():
+            send_right(z, n)
+
+        @pl.when(held_left)
+        def _():
+            send_left(z, n)
 
         return carry
 
@@ -164,7 +213,9 @@
 
     fir(0, 0)
     pl.semaphore_wait(
-        barrier, jnp.where(z < ntm - 1, 1, 0) + jnp.where(z > 0, 1, 0) + (nch - 1)
+        barrier,
+        jnp.where(z < ntm - 1, 1, 0) + jnp.where(z > 0, 1, 0) + (nch - 1)
+        + (jnp.where(is_helper, nch - 1, 0) + (share - 1) if lend else 0),
     )
     send_own(0, 0)
     lax.fori_loop(1, nblk, fir_next, 0)
@@ -193,46 +244,81 @@
         shaped[:, cols] = skewed[...].astype(jnp.bfloat16)
         return carry
 
-    lax.fori_loop(0, local // LANE, shape_cols, 0)
-
-    cut = min(LANE, tlen) * group
-    parts = [(0, cut), (cut, tlen * group - cut)]
-
-    def lend_copy(p, peer):
-        cols = pl.ds(pl.multiple_of(inward * rows, rows), rows)
-        lines = pl.ds(*parts[p])
+    lines = tlen * group // share
+    cuts = [lines // 16 * j // LOANS * 16 for j in range(LOANS)] + [lines]
+
+    def loan_lines(owner, j):
+        return pl.ds(pl.multiple_of(owner * lines + cuts[j], 16), cuts[j + 1] - cuts[j])
+
+    def loan(j, peer):
+        owner = lax.rem(p, share)
+        at = loan_lines(owner, j)
         return pltpu.make_async_remote_copy(
-            src_ref=shaped.at[lines, cols],
-            dst_ref=guest.at[lines, :],
-            send_sem=guest_sem.at[0, p],
-            recv_sem=guest_sem.at[1, p],
+            src_ref=shaped.at[at, pl.ds(pl.multiple_of(lent * rows, rows), rows)],
+            dst_ref=guest.at[at, :],
+            send_sem=loan_send.at[j],
+            recv_sem=loan_recv.at[j],
             device_id={"tmpl": peer},
             device_id_type=MESH,
         )
 
-    def gsum_copy(peer):
+    def relay(e, j, owner):
+        at = loan_lines(owner, j)
         return pltpu.make_async_remote_copy(
-            src_ref=gacc.at[:, pl.ds(BLK, total)],
-            dst_ref=gsum,
-            send_sem=gsum_sem.at[0],
-            recv_sem=gsum_sem.at[1],
+            src_ref=guest.at[at, :],
+            dst_ref=guest.at[at, :],
+            send_sem=relay_send.at[e, j],
+            recv_sem=relay_recv.at[e, j],
+            device_id={"parts": lax.rem(p + e, npt)},
+            device_id_type=MESH,
+        )
+
+    def offs_copy(peer):
+        return pltpu.make_async_remote_copy(
+            src_ref=own_offs,
+            dst_ref=guest_offs,
+            send_sem=offs_sem.at[0],
+            recv_sem=offs_sem.at[1],
             device_id={"tmpl": peer},
             device_id_type=MESH,
         )
-
-    if lend:
-        @pl.when(is_end)
-        def _():
-            lend_copy(0, inward).start()
-            lend_copy(1, inward).start()
 
     offs = jnp.zeros((group, 1), jnp.int32)
     index = lax.broadcasted_iota(jnp.int32, (group, 1), 0)
     for k in range(group):
         offs = jnp.where(index == k, offs_ref[k], offs)
 
-    def shift_rows(x):
-        amount = jnp.broadcast_to(offs, x.shape)
+    per = width // LANE
+    if lend:
+        @pl.when(is_end)
+        def _():
+            own_offs[...] = jnp.broadcast_to(offs, own_offs.shape)
+            first = lent * (rows // LANE)
+            lax.fori_loop(first, first + rows // LANE, shape_cols, 0)
+            for j in range(LOANS):
+                loan(j, inward).start()
+            offs_copy(inward).start()
+
+    lax.fori_loop(near * per, near * per + per, shape_cols, 0)
+
+    def shape_rest():
+        first = (1 - near) * per
+
+        def body(i, carry):
+            if lend:
+                skip = is_end & (lax.div(i, rows // LANE) == lent)
+
+                @pl.when(jnp.logical_not(skip))
+                def _():
+                    shape_cols(i, 0)
+            else:
+                shape_cols(i, 0)
+            return carry
+
+        lax.fori_loop(first, first + per, body, 0)
+
+    def shift_rows(x, by):
+        amount = jnp.broadcast_to(by, x.shape)
         bit = 1
         while bit < SPAN - tlen + 1:
             x = jnp.where((amount & bit) != 0, left(x, bit), x)
@@ -302,30 +388,40 @@
                 place += width
             window = window + left(window, width)
             width *= 2
-        spread(shift_rows(energy), en_out, en_in, en_send, en_recv)
-
-    def arrive(d, n):
-        near = lend if d == 1 else 0
-
-        @pl.when((z - d >= 0) & (z < ntm - near))
+        spread(shift_rows(energy, offs), en_out, en_in, en_send, en_recv)
+
+    def arrive(d, n, same):
+        def fits(src):
+            return (lax.div(src, side) == near) == same
+
+        @pl.when(
+            (z - d >= 0) & fits(lax.rem(z - d + ntm, ntm))
+            & ((z < ntm - 1) if lend and d == 2 else True)
+        )
         def _():
             src = lax.rem(z - d + ntm, ntm)
             for h in range(PIECES):
                 hop(src, n, h, right_sem, 1).wait_recv()
 
-                @pl.when(z < ntm - 1)
+                @pl.when(z < ntm - 1 - (1 if lend and d == 1 else 0))
                 def _():
                     hop(src, n, h, right_sem, 1).start()
 
-        @pl.when((z + d < ntm) & (z >= near))
+        @pl.when(
+            (z + d < ntm) & fits(lax.rem(z + d, ntm)) & ((z > 0) if lend and d == 2 else True)
+        )
         def _():
             src = lax.rem(z + d, ntm)
             for h in range(PIECES):
                 hop(src, n, h, left_sem, -1).wait_recv()
 
-                @pl.when(z > 0)
+                @pl.when(z > (1 if lend and d == 1 else 0))
                 def _():
                     hop(src, n, h, left_sem, -1).start()
+
+    def arrive_far(n):
+        for d in range(2, ntm):
+            arrive(d, n, False)
 
     def skew(n, weights, samples, acc, begin, end):
         prod[: weights.shape[0], :] = jnp.dot(
@@ -355,73 +451,133 @@
         at = pl.ds(pl.multiple_of(n * BLK, BLK), 2 * BLK)
         acc[:, at] = acc[:, at] + total_acc
 
-    def guest_block(p, n, carry):
-        line, count = parts[p]
-        weights = guest[line : line + count, :]
-        skew(n, weights, chunk(z, n)[...], gacc, line // group, (line + count) // group)
-        return carry
-
-    def block(n, carry):
-        for d in range(max(1, ntm // 2), ntm):
-            arrive(d, n)
-
-        @pl.when(n == min(1, nblk - 1))
-        def _():
-            for d in range(max(1, ntm // 2), ntm):
+    def half_block(which, n):
+        at = pl.ds(pl.multiple_of(which * width, width), width)
+        skew(n, shaped[:, at], rall[n, at, :], qacc, 0, tlen)
+
+    def guest_block(n, carry):
+        skew(n, guest[...], chunk(lent, n)[...], gacc, 0, tlen)
+        return carry
+
+    def guest_copy(d, peer):
+        other = lax.rem(c + d, nch)
+        return pltpu.make_async_remote_copy(
+            src_ref=guest_out.at[other],
+            dst_ref=guest_in.at[d],
+            send_sem=guest_send.at[d],
+            recv_sem=guest_recv.at[d],
+            device_id={"chan": other, "tmpl": peer},
+            device_id_type=MESH,
+        )
+
+    def near_round(n, carry):
+        for d in range(1, side):
+            arrive(d, n, True)
+
+        @pl.when(n == 0)
+        def _():
+            unit_arrive(1)
+
+        if side < ntm and lead < nblk:
+            @pl.when(n >= lead)
+            def _():
+                arrive_far(n - lead)
+
+        @pl.when(n == nblk - 1)
+        def _():
+            lax.fori_loop(lead, nblk, send_held, 0)
+            if ntm > 2:
+                unit_arrive(2)
+
+        half_block(near, n)
+        if side < ntm:
+            @pl.when(n == 0)
+            def _():
+                shape_rest()
+
+        return carry
+
+    def far_round(n, carry):
+        @pl.when(n < lead)
+        def _():
+            arrive(1, n, False)
+
+        @pl.when(n >= (nblk - lead if lead < nblk else 0))
+        def _():
+            arrive_far(n)
+
+        @pl.when(n == min(2, nblk - 1))
+        def _():
+            for d in range(3, ntm):
                 unit_arrive(d)
             send_energy()
 
         if lend:
-            @pl.when((n == nblk - 1) & is_helper)
+            for j in range(LOANS):
+                @pl.when(is_helper & (n == max(0, nblk - LOANS + j)))
+                def _():
+                    loan(j, outward).wait_recv()
+                    for e in range(1, share):
+                        relay(e, j, p).start()
+
+        @pl.when((n < lead) | jnp.logical_not(is_helper))
+        def _():
+            half_block(1 - near, n)
+
+        return carry
+
+    def last_round(n, carry):
+        arrive(1, n, False)
+
+        @pl.when(is_helper)
+        def _():
+            guest_block(n, 0)
+
+            @pl.when(n == nblk - 1)
             def _():
-                gacc[...] = jnp.zeros_like(gacc)
-                lend_copy(0, outward).wait_recv()
-                lax.fori_loop(0, nblk, functools.partial(guest_block, 0), 0)
-
-        skew(n, shaped[...], rall[n], qacc, 0, tlen)
-        return carry
-
-    def step(d):
-        def body(n, carry):
-            arrive(d, n)
-
-            @pl.when(n == 0)
-            def _():
-                unit_arrive(d)
-
-            return carry
-
-        lax.fori_loop(0, nblk, body, 0)
-
-    for d in range(1, max(1, ntm // 2)):
-        step(d)
-    lax.fori_loop(0, nblk, block, 0)
+                moved = shift_rows(gacc[:, BLK:], guest_offs[:, :1])
+                lag = guest_out.shape[2]
+                for j in range(nch):
+                    guest_out[j] = moved[:, j * lag : (j + 1) * lag]
+                for d in range(nch):
+                    guest_copy(d, outward).start()
+
+            half_block(1 - near, n)
+
+        return carry
+
+    lax.fori_loop(0, nblk, near_round, 0)
+    if side < ntm:
+        lax.fori_loop(0, nblk, far_round, 0)
+    else:
+        for d in range(3, ntm):
+            unit_arrive(d)
+        send_energy()
 
     if lend:
         @pl.when(is_helper)
         def _():
-            lend_copy(1, outward).wait_recv()
-            lax.fori_loop(0, nblk, functools.partial(guest_block, 1), 0)
-            gsum_copy(outward).start()
-
-        @pl.when(is_end)
-        def _():
-            gsum_copy(inward).wait_recv()
-            qacc[:, BLK:] = qacc[:, BLK:] + gsum[...]
-
-    spread(shift_rows(qacc[:, BLK:]), num_out, num_in, num_send, num_recv)
-    energy = collect(en_out, en_in, en_send, en_recv)
-    numerator = collect(num_out, num_in, num_send, num_recv)
-    out_ref[...] = numerator / jnp.sqrt(energy)
+            offs_copy(outward).wait_recv()
+            for j in range(LOANS):
+                for e in range(1, share):
+                    relay(e, j, lax.rem(p - e + npt, npt)).wait_recv()
+            lax.fori_loop(0, lead, guest_block, 0)
+
+        lax.fori_loop(lead, nblk, last_round, 0)
+
+    spread(shift_rows(qacc[:, BLK:], offs), num_out, num_in, num_send, num_recv)
 
     def drain(n, carry):
         for s in range(ntm):
-            @pl.when((s <= z) & (z < ntm - 1) & ((s != z) | (z < ntm - 1 - lend)))
+            @pl.when(
+                (s <= z) & (z < ntm - 1)
+                & (((z != ntm - 2) | (s != ntm - 3)) if lend else True)
+            )
             def _():
                 for h in range(PIECES):
                     hop(s, n, h, right_sem, 1).wait_send()
 
-            @pl.when((s >= z) & (z > 0) & ((s != z) | (z > lend)))
+            @pl.when((s >= z) & (z > 0) & (((z != 1) | (s != 2)) if lend else True))
             def _():
                 for h in range(PIECES):
                     hop(s, n, h, left_sem, -1).wait_send()
@@ -441,12 +597,36 @@
     if lend:
         @pl.when(is_end)
         def _():
-            lend_copy(0, inward).wait_send()
-            lend_copy(1, inward).wait_send()
+            for j in range(LOANS):
+                loan(j, inward).wait_send()
+            offs_copy(inward).wait_send()
 
         @pl.when(is_helper)
         def _():
-            gsum_copy(outward).wait_send()
+            for j in range(LOANS):
+                for e in range(1, share):
+                    relay(e, j, p).wait_send()
+
+    energy = collect(en_out, en_in, en_send, en_recv)
+    numerator = collect(num_out, num_in, num_send, num_recv)
+    if lend:
+        num_out[0] = numerator
+
+        @pl.when(is_end)
+        def _():
+            total_in = num_out[0]
+            for d in range(nch):
+                guest_copy(d, inward).wait_recv()
+                total_in = total_in + guest_in[d]
+            num_out[0] = total_in
+
+        @pl.when(is_helper)
+        def _():
+            for d in range(nch):
+                guest_copy(d, outward).wait_send()
+
+        numerator = num_out[0]
+    out_ref[...] = numerator / jnp.sqrt(energy)
 
 
 def shards(raw_traces, filter_taps, templates, offsets, channel_mask):
@@ -458,12 +638,15 @@
     total = nblk * BLK
     lag = (total - SPAN) // nch
     nun = rows // min(LANE, rows)
-    lend = int(ntm >= 4 and rows % LANE == 0 and tlen > LANE)
+    npt = lax.axis_size("parts")
+    lend = int(ntm == 4 and rows % LANE == 0 and nblk >= LOANS)
+    share = npt if lend and group * tlen % (16 * npt) == 0 else 1
+    lead = min(LEAD, nblk - 1) if lend else nblk
     f32, bf16, dma = jnp.float32, jnp.bfloat16, pltpu.SemaphoreType.DMA
     any_spec = pl.BlockSpec(memory_space=pl.ANY)
     vmem_spec = pl.BlockSpec(memory_space=pltpu.VMEM)
     return pl.pallas_call(
-        functools.partial(kernel, ntm, nch, lend),
+        functools.partial(kernel, ntm, nch, npt, lend, share, lead),
         out_shape=jax.ShapeDtypeStruct((group, lag), f32),
         in_specs=[
             any_spec, any_spec, any_spec, any_spec, any_spec,
@@ -488,7 +671,10 @@
             pltpu.VMEM((nch, group, lag), f32),
             pltpu.VMEM((group * tlen, rows if lend else LANE), bf16),
             pltpu.VMEM((group, BLK + total), f32),
-            pltpu.VMEM((group, total), f32),
+            pltpu.VMEM((nch, group, lag), f32),
+            pltpu.VMEM((nch, group, lag), f32),
+            pltpu.VMEM((group, LANE), jnp.int32),
+            pltpu.VMEM((group, LANE), jnp.int32),
             dma((4,)),
             dma((nblk,)),
             dma((ntm, nblk * PIECES)),
@@ -501,8 +687,13 @@
             dma((nch,)),
             dma((nch,)),
             dma((nch,)),
-            dma((2, 2)),
+            dma((LOANS,)),
+            dma((LOANS,)),
+            dma((npt, LOANS)),
+            dma((npt, LOANS)),
             dma((2,)),
+            dma((nch,)),
+            dma((nch,)),
         ],
         compiler_params=pltpu.CompilerParams(
             collective_id=0, has_side_effects=True, vmem_limit_bytes=60 * 1024 * 1024

time: 50 us -> 46 us (0.920)
  Pallas kernels: 48.5 us -> 44.5 us
    pallas_call x1, Pallas kernels: 48.5 us -> 44.5 us  [shards(): pl.pallas_call(functools.partial(kernel, ntm, nch, npt, lend, share, lead...]
where the time goes in v1:
time: 46 us; the launch traced here: 45.8 us
  Pallas kernels  44.5 us (97%)
  local copies, waits for them, and re-layouts  1.3 us (3%)
    pallas_call x1, Pallas kernels, shards(): pl.pallas_call(functools.partial(kernel, ntm, nch, npt, lend, share, lead...  44.5 us
    unnamed x1, local copies, waits for them, and re-layouts  1.3 us

profile of v1, /device:TPU:0, one launch (start us, length us, event | category | flops | bytes accessed | tf_op | source)
XLA Modules:
  0.0 45.8 jit_solution(17506662789938423517)
XLA Ops:
  0.0 44.5 %shard_map.55 = f32[8,256]{1,0:T(8,128)} custom-call(f32[256,1408]{1,0:T(8,128)} %raw_hbm.1, f32[1,129]{1,0:T(1,128)} %bitcast.1, bf16[8,200,1024]{2,1,0:T(8,128)(2,1)} %tmpl_hbm.1, s32[8,4096]{1,0:T(8,128)} %mask_hbm.1, s32[8]{0:T(128)} %offs_hbm.1), custom_call_target="tpu_custom_call" | custom-call | tf_op jit(solution)/shard_map/pallas_call | solution.py:648
  44.5 1.3 %copy.7 = f32[8,256]{1,0:T(8,128)} copy(f32[8,256]{1,0:T(8,128)} %shard_map.55) | data formatting | bytes 16384

commit v2 on v1

--- a/solution.py
+++ b/solution.py
@@ -13,7 +13,7 @@
 MESH = pl.DeviceIdType.MESH
 PIECES = 1
 LEAD = 3
-LOANS = 4
+LOANS = (16, 16, 15, 14, 13, 11, 9, 6)
 
 
 def left(x, count):
@@ -229,7 +229,6 @@
         unit_hop(z, unit_left, -1).start()
 
     lax.fori_loop(1, nblk, send_own, 0)
-
     for item in loads:
         item.wait()
 
@@ -245,7 +244,8 @@
         return carry
 
     lines = tlen * group // share
-    cuts = [lines // 16 * j // LOANS * 16 for j in range(LOANS)] + [lines]
+    npc = len(LOANS)
+    cuts = [lines // 16 * sum(LOANS[:j]) // sum(LOANS) * 16 for j in range(npc)] + [lines]
 
     def loan_lines(owner, j):
         return pl.ds(pl.multiple_of(owner * lines + cuts[j], 16), cuts[j + 1] - cuts[j])
@@ -289,17 +289,20 @@
         offs = jnp.where(index == k, offs_ref[k], offs)
 
     per = width // LANE
+    ahead = rows // LANE if lend else 0
+    if lend:
+        first = jnp.where(is_end, lent * ahead, near * per)
+        lax.fori_loop(first, first + ahead, shape_cols, 0)
+        own_offs[...] = jnp.broadcast_to(offs, own_offs.shape)
+
     if lend:
         @pl.when(is_end)
         def _():
-            own_offs[...] = jnp.broadcast_to(offs, own_offs.shape)
-            first = lent * (rows // LANE)
-            lax.fori_loop(first, first + rows // LANE, shape_cols, 0)
-            for j in range(LOANS):
+            for j in range(npc):
                 loan(j, inward).start()
             offs_copy(inward).start()
 
-    lax.fori_loop(near * per, near * per + per, shape_cols, 0)
+    lax.fori_loop(near * per + jnp.where(is_end, 0, ahead), near * per + per, shape_cols, 0)
 
     def shape_rest():
         first = (1 - near) * per
@@ -428,7 +431,9 @@
             weights, samples, preferred_element_type=jnp.float32
         )
         blank = jnp.zeros((group, LANE), jnp.float32)
-        total_acc = jnp.zeros((group, 2 * BLK), jnp.float32)
+        span = end - begin
+        reach = BLK + (2 * LANE if span > LANE else LANE)
+        total_acc = jnp.zeros((group, reach), jnp.float32)
 
         def row(tap):
             if tap < begin or tap >= end:
@@ -436,7 +441,7 @@
             line = (tap - begin) * group
             return prod[line : line + group, :]
 
-        for g in range(min(LANE, tlen)):
+        for g in range(min(LANE, span)):
             low, high = row(g), row(g + LANE)
             if low is None and high is None:
                 continue
@@ -446,9 +451,12 @@
             if high is not None:
                 carry_in = high[:, :LANE]
                 first = high[:, LANE:] if low is None else first + high[:, LANE:]
-            wide = jnp.concatenate([blank, carry_in, first, second], axis=1)
+            if span > LANE:
+                wide = jnp.concatenate([blank, carry_in, first, second], axis=1)
+            else:
+                wide = jnp.concatenate([blank, first, second], axis=1)
             total_acc = total_acc + left(wide, g)
-        at = pl.ds(pl.multiple_of(n * BLK, BLK), 2 * BLK)
+        at = pl.ds(pl.multiple_of(n * BLK + 2 * BLK - reach, LANE), reach)
         acc[:, at] = acc[:, at] + total_acc
 
     def half_block(which, n):
@@ -456,8 +464,12 @@
         skew(n, shaped[:, at], rall[n, at, :], qacc, 0, tlen)
 
     def guest_block(n, carry):
-        skew(n, guest[...], chunk(lent, n)[...], gacc, 0, tlen)
-        return carry
+        skew(n, guest[...], chunk(lent, n)[...], gacc.at[0], 0, tlen)
+        return carry
+
+    def guest_share(owner, n):
+        at = pl.ds(pl.multiple_of(owner * lines, 16), lines)
+        skew(n, guest[at, :], chunk(lent, n)[...], gacc.at[owner], 0, tlen // share)
 
     def guest_copy(d, peer):
         other = lax.rem(c + d, nch)
@@ -512,39 +524,36 @@
                 unit_arrive(d)
             send_energy()
 
+        @pl.when((n < lead) | jnp.logical_not(is_helper))
+        def _():
+            half_block(1 - near, n)
+
         if lend:
-            for j in range(LOANS):
-                @pl.when(is_helper & (n == max(0, nblk - LOANS + j)))
+            for j in range(npc):
+                @pl.when(is_helper & (n == min(nblk - 1, 1 + (2 * j + 1) * 8 // (5 * npc))))
                 def _():
                     loan(j, outward).wait_recv()
                     for e in range(1, share):
                         relay(e, j, p).start()
 
-        @pl.when((n < lead) | jnp.logical_not(is_helper))
-        def _():
-            half_block(1 - near, n)
-
-        return carry
-
-    def last_round(n, carry):
+        return carry
+
+    def held_round(n, carry):
         arrive(1, n, False)
-
-        @pl.when(is_helper)
-        def _():
-            guest_block(n, 0)
-
-            @pl.when(n == nblk - 1)
-            def _():
-                moved = shift_rows(gacc[:, BLK:], guest_offs[:, :1])
-                lag = guest_out.shape[2]
-                for j in range(nch):
-                    guest_out[j] = moved[:, j * lag : (j + 1) * lag]
-                for d in range(nch):
-                    guest_copy(d, outward).start()
-
-            half_block(1 - near, n)
-
-        return carry
+        half_block(1 - near, n)
+        return carry
+
+    def finish_guest():
+        moved = gacc[0, :, BLK:]
+        if share > 1:
+            for q in range(1, share):
+                moved = moved + left(gacc[q], q * tlen // share)[:, BLK:]
+        moved = shift_rows(moved, guest_offs[:, :1])
+        lag = guest_out.shape[2]
+        for j in range(nch):
+            guest_out[j] = moved[:, j * lag : (j + 1) * lag]
+        for d in range(nch):
+            guest_copy(d, outward).start()
 
     lax.fori_loop(0, nblk, near_round, 0)
     if side < ntm:
@@ -557,13 +566,28 @@
     if lend:
         @pl.when(is_helper)
         def _():
+            def body(n, carry):
+                guest_share(lax.rem(p, share), n)
+                return carry
+
+            lax.fori_loop(0, lead, body, 0)
+            lax.fori_loop(lead, nblk - 1, held_round, 0)
+            for e in range(1, share):
+                owner = lax.rem(p - e + npt, npt)
+                for j in range(npc):
+                    relay(e, j, owner).wait_recv()
+
+                def other(n, carry):
+                    guest_share(owner, n)
+                    return carry
+
+                lax.fori_loop(0, lead, other, 0)
             offs_copy(outward).wait_recv()
-            for j in range(LOANS):
-                for e in range(1, share):
-                    relay(e, j, lax.rem(p - e + npt, npt)).wait_recv()
-            lax.fori_loop(0, lead, guest_block, 0)
-
-        lax.fori_loop(lead, nblk, last_round, 0)
+            lax.fori_loop(lead, nblk - 1, guest_block, 0)
+            arrive(1, nblk - 1, False)
+            guest_block(nblk - 1, 0)
+            finish_guest()
+            half_block(1 - near, nblk - 1)
 
     spread(shift_rows(qacc[:, BLK:], offs), num_out, num_in, num_send, num_recv)
 
@@ -597,13 +621,13 @@
     if lend:
         @pl.when(is_end)
         def _():
-            for j in range(LOANS):
+            for j in range(npc):
                 loan(j, inward).wait_send()
             offs_copy(inward).wait_send()
 
         @pl.when(is_helper)
         def _():
-            for j in range(LOANS):
+            for j in range(npc):
                 for e in range(1, share):
                     relay(e, j, p).wait_send()
 
@@ -639,8 +663,8 @@
     lag = (total - SPAN) // nch
     nun = rows // min(LANE, rows)
     npt = lax.axis_size("parts")
-    lend = int(ntm == 4 and rows % LANE == 0 and nblk >= LOANS)
-    share = npt if lend and group * tlen % (16 * npt) == 0 else 1
+    lend = int(ntm == 4 and rows % LANE == 0 and nblk >= 3)
+    share = npt if lend and tlen % npt == 0 and group * tlen % (16 * npt) == 0 else 1
     lead = min(LEAD, nblk - 1) if lend else nblk
     f32, bf16, dma = jnp.float32, jnp.bfloat16, pltpu.SemaphoreType.DMA
     any_spec = pl.BlockSpec(memory_space=pl.ANY)
@@ -670,7 +694,7 @@
             pltpu.VMEM((nch, group, lag), f32),
             pltpu.VMEM((nch, group, lag), f32),
             pltpu.VMEM((group * tlen, rows if lend else LANE), bf16),
-            pltpu.VMEM((group, BLK + total), f32),
+            pltpu.VMEM((share, group, BLK + total), f32),
             pltpu.VMEM((nch, group, lag), f32),
             pltpu.VMEM((nch, group, lag), f32),
             pltpu.VMEM((group, LANE), jnp.int32),
@@ -687,10 +711,10 @@
             dma((nch,)),
             dma((nch,)),
             dma((nch,)),
-            dma((LOANS,)),
-            dma((LOANS,)),
-            dma((npt, LOANS)),
-            dma((npt, LOANS)),
+            dma((len(LOANS),)),
+            dma((len(LOANS),)),
+            dma((npt, len(LOANS))),
+            dma((npt, len(LOANS))),
             dma((2,)),
             dma((nch,)),
             dma((nch,)),

time: 46 us -> 44.5 us (0.967)
  Pallas kernels: 44.5 us -> 43 us
    pallas_call x1, Pallas kernels: 44.5 us -> 43 us  [shards(): pl.pallas_call(functools.partial(kernel, ntm, nch, npt, lend, share, lead...]
where the time goes in v2:
time: 44.5 us; the launch traced here: 44.3 us
  Pallas kernels  43 us (97%)
  local copies, waits for them, and re-layouts  1.3 us (3%)
    pallas_call x1, Pallas kernels, shards(): pl.pallas_call(functools.partial(kernel, ntm, nch, npt, lend, share, lead...  43 us
    unnamed x1, local copies, waits for them, and re-layouts  1.3 us

profile of v2, /device:TPU:0, one launch (start us, length us, event | category | flops | bytes accessed | tf_op | source)
XLA Modules:
  0.0 44.3 jit_solution(12603362477348824777)
XLA Ops:
  0.0 43.0 %shard_map.55 = f32[8,256]{1,0:T(8,128)} custom-call(f32[256,1408]{1,0:T(8,128)} %raw_hbm.1, f32[1,129]{1,0:T(1,128)} %bitcast.1, bf16[8,200,1024]{2,1,0:T(8,128)(2,1)} %tmpl_hbm.1, s32[8,4096]{1,0:T(8,128)} %mask_hbm.1, s32[8]{0:T(128)} %offs_hbm.1), custom_call_target="tpu_custom_call" | custom-call | tf_op jit(solution)/shard_map/pallas_call | solution.py:672
  43.0 1.3 %copy.7 = f32[8,256]{1,0:T(8,128)} copy(f32[8,256]{1,0:T(8,128)} %shard_map.55) | data formatting | bytes 16384

commit v3 on v2

--- a/solution.py
+++ b/solution.py
@@ -530,7 +530,7 @@
 
         if lend:
             for j in range(npc):
-                @pl.when(is_helper & (n == min(nblk - 1, 1 + (2 * j + 1) * 8 // (5 * npc))))
+                @pl.when(is_helper & (n == min(nblk - 1, 1 + (2 * j + 1) * 6 // (5 * npc))))
                 def _():
                     loan(j, outward).wait_recv()
                     for e in range(1, share):
@@ -571,7 +571,12 @@
                 return carry
 
             lax.fori_loop(0, lead, body, 0)
-            lax.fori_loop(lead, nblk - 1, held_round, 0)
+            def held_share(n, carry):
+                arrive(1, n, False)
+                guest_share(lax.rem(p, share), n)
+                return carry
+
+            lax.fori_loop(lead, nblk - 1, held_share, 0)
             for e in range(1, share):
                 owner = lax.rem(p - e + npt, npt)
                 for j in range(npc):
@@ -581,13 +586,21 @@
                     guest_share(owner, n)
                     return carry
 
-                lax.fori_loop(0, lead, other, 0)
+                lax.fori_loop(0, nblk - 1, other, 0)
             offs_copy(outward).wait_recv()
-            lax.fori_loop(lead, nblk - 1, guest_block, 0)
-            arrive(1, nblk - 1, False)
-            guest_block(nblk - 1, 0)
+
+            def held_guest(n, carry):
+                arrive(1, n, False)
+                guest_block(n, 0)
+                return carry
+
+            def held_own(n, carry):
+                half_block(1 - near, n)
+                return carry
+
+            held_guest(nblk - 1, 0)
             finish_guest()
-            half_block(1 - near, nblk - 1)
+            lax.fori_loop(lead, nblk, held_own, 0)
 
     spread(shift_rows(qacc[:, BLK:], offs), num_out, num_in, num_send, num_recv)
 
@@ -671,7 +684,7 @@
     vmem_spec = pl.BlockSpec(memory_space=pltpu.VMEM)
     return pl.pallas_call(
         functools.partial(kernel, ntm, nch, npt, lend, share, lead),
-        out_shape=jax.ShapeDtypeStruct((group, lag), f32),
+        out_shape=pltpu.VMEM((group, lag), f32),
         in_specs=[
             any_spec, any_spec, any_spec, any_spec, any_spec,
         ],

time: 44.5 us -> 42.5 us (0.955)
  Pallas kernels: 43 us -> 41.8 us
  local copies, waits for them, and re-layouts: 1.3 us -> 0.6 us
    pallas_call x1, Pallas kernels: 43 us -> 41.8 us  [shards(): pl.pallas_call(functools.partial(kernel, ntm, nch, npt, lend, share, lead...]
    unnamed x1, local copies, waits for them, and re-layouts: 1.3 us -> 0.6 us
where the time goes in v3:
time: 42.5 us; the launch traced here: 42.4 us
  Pallas kernels  41.8 us (98%)
  local copies, waits for them, and re-layouts  0.6 us (1%)
    pallas_call x1, Pallas kernels, shards(): pl.pallas_call(functools.partial(kernel, ntm, nch, npt, lend, share, lead...  41.8 us

profile of v3, /device:TPU:0, one launch (start us, length us, event | category | flops | bytes accessed | tf_op | source)
XLA Modules:
  0.0 42.4 jit_solution(11292827408307739401)
XLA Ops:
  0.0 41.8 %shard_map.55 = f32[8,256]{1,0:T(8,128)S(1)} custom-call(f32[256,1408]{1,0:T(8,128)} %raw_hbm.1, f32[1,129]{1,0:T(1,128)} %bitcast.1, bf16[8,200,1024]{2,1,0:T(8,128)(2,1)} %tmpl_hbm.1, s32[8,4096]{1,0:T(8,128)} %mask_hbm.1, s32[8]{0:T(128)} %offs_hbm.1), custom_call_target="tpu_custom_call" | custom-call | tf_op jit(solution)/shard_map/pallas_call | solution.py:685
  41.8 0.6 %copy.7 = f32[8,256]{1,0:T(8,128)} copy(f32[8,256]{1,0:T(8,128)S(1)} %shard_map.55) | data formatting | bytes 16384

commit v4 on v3

--- a/solution.py
+++ b/solution.py
@@ -324,8 +324,13 @@
         amount = jnp.broadcast_to(by, x.shape)
         bit = 1
         while bit < SPAN - tlen + 1:
-            x = jnp.where((amount & bit) != 0, left(x, bit), x)
-            bit *= 2
+            digit = (amount // bit) & 3
+            y = x
+            for step in range(1, 4):
+                if step * bit <= SPAN - tlen:
+                    y = jnp.where(digit == step, left(x, step * bit), y)
+            x = y
+            bit *= 4
         return x
 
     def spread(x, own_ref, in_ref, send, recv):

time: 42.5 us -> 42.4 us (level)
  no operation moved by 1% of the time
where the time goes in v4:
time: 42.4 us; the launch traced here: 42.2 us
  Pallas kernels  41.6 us (98%)
  local copies, waits for them, and re-layouts  0.6 us (1%)
    pallas_call x1, Pallas kernels, shards(): pl.pallas_call(functools.partial(kernel, ntm, nch, npt, lend, share, lead...  41.6 us

profile of v4, /device:TPU:0, one launch (start us, length us, event | category | flops | bytes accessed | tf_op | source)
XLA Modules:
  0.0 42.2 jit_solution(11257232406313971717)
XLA Ops:
  0.0 41.6 %shard_map.55 = f32[8,256]{1,0:T(8,128)S(1)} custom-call(f32[256,1408]{1,0:T(8,128)} %raw_hbm.1, f32[1,129]{1,0:T(1,128)} %bitcast.1, bf16[8,200,1024]{2,1,0:T(8,128)(2,1)} %tmpl_hbm.1, s32[8,4096]{1,0:T(8,128)} %mask_hbm.1, s32[8]{0:T(128)} %offs_hbm.1), custom_call_target="tpu_custom_call" | custom-call | tf_op jit(solution)/shard_map/pallas_call | solution.py:690
  41.6 0.6 %copy.7 = f32[8,256]{1,0:T(8,128)} copy(f32[8,256]{1,0:T(8,128)S(1)} %shard_map.55) | data formatting | bytes 16384
